TPU v7x, 512 devices: a whole 4x4x16 slice. The times are simulated.
512 devices in a mesh: space: 64 (over y_hi, z, core), tm: 8 (over y_lo, x).
Axes of the slice: x: 4, y: 4 (y_hi: 2, y_lo: 2; y = y_hi * 2 + y_lo), z: 16, core: 2. Of those that a mesh axis runs over, the one named last changes fastest.
Arguments:
- row_orbitals: bfloat16 [32768, 2048], P('space', 'tm'), may hold values from -0.890625 to 0.890625
- column_orbitals: bfloat16 [1024, 2048], P('space', 'tm'), may hold values from -0.890625 to 0.890625
- occupation: int32 [2048], replicated, may hold values from 0 to 2
- order: int32 [2048], replicated, may hold values from 0 to 2047, each once
- levels: float32 [2048], replicated, may hold values from 0.1 to 1
- times: float32 [8], replicated, may hold values from 0.05 to 1.5
- quad_weights: float32 [8], replicated, may hold values from 0.5 to 1.5
- freqs: float32 [8], replicated, may hold values from 0.1 to 4
Outputs:
- spectrum: float32 [8, 32768, 1024], P(None, ('space', 'tm'))
Inputs may be any that keep to these rules, and one draw needn't show every extreme that they name: `order`: each index of 0 to 2047 once.
All inputs are finite; a program needn't handle non-finite values.
Results may differ from a plain program's by a relative error of at most 0.0026.
Values may be sent and summed in bfloat16 or wider, within the bound.
A program may use at most 64 MiB of HBM per device.

v0:
```python
import jax
import jax.numpy as jnp
from jax import lax
from jax.sharding import PartitionSpec as P


def in_order(tiles, dim):
    dims = list(tiles.shape[1:])
    dims[dim] *= tiles.shape[0]
    return jnp.moveaxis(tiles, 0, dim).reshape(dims)


def from_everyone(value, axis):
    copies = jnp.broadcast_to(value, (lax.axis_size(axis), *value.shape))
    return lax.all_to_all(copies, axis, split_axis=0, concat_axis=0, tiled=True)


def gather_directly(value, axis, dim):
    return in_order(from_everyone(value, axis), dim)


def body(row_orbitals, column_orbitals, occupation, order, levels, times, quad_weights, freqs):
    energy = jnp.take(levels, order)
    filled = occupation.astype(jnp.float32) * 0.5
    rows_full = lax.all_to_all(row_orbitals, "tm", split_axis=0, concat_axis=1, tiled=True)
    decays = jnp.exp(-times[:, None] * energy[None, :])
    full_weight = filled[None, :] * decays
    empty_weight = (1.0 - filled)[None, :] * decays
    row_values = rows_full.astype(jnp.float32)[None]
    scaled_full = (row_values * full_weight[:, None, :]).astype(jnp.bfloat16)
    scaled_empty = (row_values * empty_weight[:, None, :]).astype(jnp.bfloat16)
    orbital_count = rows_full.shape[1]
    half_rows = scaled_full.shape[0] * scaled_full.shape[1]
    stacked = jnp.concatenate(
        (
            scaled_full.reshape(half_rows, orbital_count),
            scaled_empty.reshape(half_rows, orbital_count),
        ),
        axis=0,
    )
    col_count = column_orbitals.shape[0] * lax.axis_size("space")
    partial_value = gather_directly(column_orbitals, "space", 0)
    columns = lax.all_gather(partial_value, "tm", axis=1, tiled=True)
    greens = lax.dot_general(
        stacked, columns, (((1,), (1,)), ((), ())), preferred_element_type=jnp.float32
    )
    product = (greens[:half_rows] * greens[half_rows:]).astype(jnp.bfloat16)
    time_count = times.shape[0]
    gathered = product.reshape(time_count, half_rows // time_count, col_count)
    sub_rows = gathered.shape[1]
    cosines = quad_weights[None, :] * jnp.cos(freqs[:, None] * times[None, :])
    spectrum = jnp.dot(
        cosines,
        gathered.reshape(time_count, sub_rows * col_count).astype(jnp.float32),
        precision=lax.Precision.HIGHEST,
    )
    return spectrum.reshape(freqs.shape[0], sub_rows, col_count)


def solution(mesh):
    placed = (P("space", "tm"), P("space", "tm"), P(), P(), P(), P(), P(), P())
    return jax.shard_map(
        body, mesh=mesh, in_specs=placed, out_specs=P(None, ("space", "tm"), None), check_vma=False
    )
```

profile of v0, /device:TPU:12, one launch (start us, length us, event | category | flops | bytes accessed | tf_op | source)
XLA Modules:
  0.0 138.9 jit_solution(8120393454277852381)
XLA Ops:
  6.5 0.0 copy-start
  6.5 0.0 all-gather.2.cloned.1.call-start
  6.5 0.7 broadcast_in_dim.12
  7.3 49.2 %all_to_all.18 = bf16[64,16,256]{2,1,0:T(8,128)(2,1)} all-to-all(bf16[64,16,256]{2,1,0:T(8,128)(2,1)S(1)} %broadcast_in_dim.12), channel_id=1, replica_groups=mesh['space'=64,'tm'=8] {'space'}, dimensions={0} | all-to-all | bytes 1048576 | tf_op jit(solution)/shard_map/all_to_all | solution.py:15
  56.5 0.0 all-gather.2.cloned.1.call-update
  56.5 5.7 %all-to-all-start = ((bf16[8,64,256]{2,1,0:T(8,128)(2,1)}), bf16[8,64,256]{2,1,0:T(8,128)(2,1)S(1)}, u32[]{:S(2)}, u32[]{:S(2)}) async-start(bf16[8,64,256]{2,1,0:T(8,128)(2,1)} %bitcast.21), calls=%async_computation | async-start | bytes 524288 | tf_op jit(solution)/shard_map/all_to_all | solution.py:25
  62.2 0.7 neg.4
  62.9 0.7 fusion.7
  63.6 0.0 copy-done
  63.6 0.0 copy-start.1
  63.6 0.0 copy-start.2
  63.6 11.8 %gather_fusion = f32[2048]{0:T(1024)S(1)} fusion(f32[2048]{0:T(1024)S(1)} %copy-done, s32[2048]{0:T(1024)S(1)} %fusion.7), kind=kCustom, calls=%fused_computation | custom fusion | bytes 24576 | tf_op jit(solution)/shard_map/jit(_take)/gather | solution.py:23
  75.4 0.0 copy-done.1
  75.4 0.0 copy-done.2
  75.4 0.1 fusion.6
  75.5 0.0 all-to-all-done
  75.6 2.3 %multiply_convert_fusion.1 = (bf16[8,64,2048]{2,1,0:T(8,128)(2,1)S(1)}, bf16[8,64,2048]{2,1,0:T(8,128)(2,1)}) fusion(f32[8,2048]{1,0:T(8,128)S(1)} %get-tuple-element.7, f32[64,2048]{1,0:T(8,128)S(1)} %bitcast.19, f32[8,2048]{1,0:T(8,128)S(1)} %get-tuple-element.8), kind=kLoop, calls=%fused_computation.6 | loop fusion | flops 4194304 | bytes 4849664 | tf_op jit(solution)/shard_map/convert_element_type | solution.py:30
  77.9 42.6 %all-gather.2.cloned.1.call-done = bf16[1024,2048]{1,0:T(8,128)(2,1)} async-done(((bf16[1024,256]{1,0:T(8,128)(2,1)}), bf16[1024,2048]{1,0:T(8,128)(2,1)}) %all-gather.2.cloned.1.call-update) | async-done | bytes 4194320 | tf_op jit(solution)/shard_map/all_gather | solution.py:43
  120.6 7.0 %fusion = f32[1024,1024]{1,0:T(8,128)S(1)} fusion(bf16[1024,2048]{1,0:T(8,128)(2,1)} %all-gather.2.cloned.1.call-done, bf16[512,2048]{1,0:T(8,128)(2,1)} %bitcast.18, bf16[512,2048]{1,0:T(8,128)(2,1)S(1)} %bitcast.17), kind=kOutput, calls=%fused_computation.1 | convolution fusion | flops 4303355904 | bytes 12582912 | tf_op jit(solution)/shard_map/dot_general | solution.py:44
  127.6 0.0 copy-start.3
  127.6 0.0 copy-start.4
  127.6 0.0 copy-start.5
  127.6 0.3 fusion.4
  127.9 0.5 reshape_reshape.3
  128.4 0.0 copy-done.3
  128.4 0.0 copy-done.4
  128.4 0.0 copy-done.5
  128.4 1.1 fusion.8
  129.6 2.5 %copy.13 = f32[8,64,1024]{2,1,0:T(8,128)} copy(f32[8,64,1024]{2,0,1:T(8,128)S(1)} %fusion.8) | data formatting | bytes 4194304 | tf_op jit(solution)/shard_map/dot_general | solution.py:52
  (3 shorter events, 0.1 us)
Async XLA Ops:
  6.5 57.0 %copy-start = (f32[2048]{0:T(1024)S(1)}, f32[2048]{0:T(1024)}, u32[]{:S(2)}) copy-start(f32[2048]{0:T(1024)} %param.12) | copy-start | bytes 24580
  6.5 114.0 %all-gather.2.cloned.1.call-start = ((), (), s32[]{:S(2)}) async-start(), calls=%async_computation.2 | async-start | bytes 4718592 | tf_op jit(solution)/shard_map/all_gather | solution.py:43
  56.5 19.0 %all-to-all-start = ((bf16[8,64,256]{2,1,0:T(8,128)(2,1)}), bf16[8,64,256]{2,1,0:T(8,128)(2,1)S(1)}, u32[]{:S(2)}, u32[]{:S(2)}) async-start(bf16[8,64,256]{2,1,0:T(8,128)(2,1)} %bitcast.21), calls=%async_computation | async-start | bytes 524288 | tf_op jit(solution)/shard_map/all_to_all | solution.py:25
  63.6 11.8 %copy-start.1 = (s32[2048]{0:T(1024)S(1)}, s32[2048]{0:T(1024)}, u32[]{:S(2)}) copy-start(s32[2048]{0:T(1024)} %param.11) | copy-start | bytes 24580
  63.6 11.8 %copy-start.2 = (s32[2048]{0:T(1024)S(1)}, s32[2048]{0:T(1024)}, u32[]{:S(2)}) copy-start(s32[2048]{0:T(1024)} %param.10) | copy-start | bytes 24580
  127.6 0.8 copy-start.3
  127.6 0.8 copy-start.4
  127.6 0.8 copy-start.5
Sparse Core Ops, SparseCore 0:
  56.6 63.8 all-gather.1
where the time goes:
time: 139 us
  blocking collectives  49.2 us (35%)
  waiting for transfers between devices  42.7 us (31%)
  local copies, waits for them, and re-layouts  15.6 us (11%)
  between operations  13.5 us (10%)
  matrix products  8.11 us (6%)
  starting transfers between devices  5.72 us (4%)
  other arithmetic  4.1 us (3%)
    all_to_all x1, blocking collectives, from_everyone(): return lax.all_to_all(copies, axis, split_axis=0, concat_axis=0, tiled=True)  49.2 us
    all_gather x1, waiting for transfers between devices, body(): columns = lax.all_gather(partial_value, 'tm', axis=1, tiled=True)  42.6 us
    gather x1, local copies, waits for them, and re-layouts, body(): energy = jnp.take(levels, order)  11.8 us
    dot_general x1, matrix products, body(): lax.dot_general(stacked, columns, (((1,), (1,)), ((), ())), preferred_ele...  7 us
    all_to_all x1, starting transfers between devices, body(): lax.all_to_all(row_orbitals, 'tm', split_axis=0, concat_axis=1, tiled=True)  5.72 us
  transfers between devices with their start and end apart: 2, of which 1 were waited for; matrix products, arithmetic and copies ran while one was open for 11% of the time, Pallas kernels for 0%

commit v1 on v0

v1 whole, which is shorter than its diff:
```python
import functools

import jax
import jax.numpy as jnp
from jax import lax
from jax.experimental import pallas as pl
from jax.experimental.pallas import tpu as pltpu
from jax.sharding import PartitionSpec as P

MESH = pl.DeviceIdType.MESH
NX, NY, NZ = 4, 4, 16


def here():
    space, tm = lax.axis_index("space"), lax.axis_index("tm")
    return tm % NX, (space // 32) * 2 + tm // NX, (space // 2) % NZ, space % 2


def device(x, y, z, core):
    return ((y // 2 * NZ + z) * 2 + core, (y % 2) * NX + x)


def position(rel):
    return 2 * rel - 1 if rel > 0 else -2 * rel


def gather_kernel(rows_hbm, columns_hbm, c_ref, r_ref, zs, zr, rs, rr, fs, fr, ss, sr, ks, kr, local):
    x, y, z, core = here()
    tm = lax.axis_index("tm")

    own = [
        pltpu.make_async_copy(columns_hbm.at[:, pl.ds(0, 128)], c_ref.at[core, 0, 0, x, y, 0], local.at[0]),
        pltpu.make_async_copy(columns_hbm.at[:, pl.ds(128, 128)], c_ref.at[core, 1, 0, y, x, 0], local.at[1]),
        pltpu.make_async_copy(rows_hbm.at[pl.ds(pl.multiple_of(tm * 64, 64), 64)], r_ref.at[tm], local.at[2]),
    ]
    for copy in own:
        copy.start()

    z_peers = [device(x, y, (z + d) % NZ, core) for d in (1, 15, 2, 14)]
    x_peers = [device((x + d) % NX, y, z, core) for d in (1, 3, 2)]
    y_peers = [device(x, (y + d) % NY, z, core) for d in (1, 3, 2)]
    y_twin = y // 2 * 2 + (1 - y % 2)
    row_peers = [device((x + dx) % NX, yy, z, core) for dx in range(NX) for yy in (y, y_twin) if dx or yy is y_twin]
    diagonal = [device((x + dx) % NX, y_twin, z, core) for dx in range(1, NX)]
    sibling = device(x, y, z, 1 - core)

    barrier = pltpu.get_barrier_semaphore()
    greeted = z_peers + x_peers + y_peers + diagonal + [sibling]
    for peer in greeted:
        pl.semaphore_signal(barrier, inc=1, device_id=peer, device_id_type=MESH)
    pl.semaphore_wait(barrier, len(greeted))

    started = []

    def send(src, dst, send_sem, recv_sem, peer):
        copy = pltpu.make_async_remote_copy(
            src_ref=src, dst_ref=dst, send_sem=send_sem, recv_sem=recv_sem, device_id=peer, device_id_type=MESH
        )
        copy.start()
        started.append(copy)
        return copy

    def spot(half, p):
        return c_ref.at[core, half, p // 4, (x, y)[half], (y, x)[half], p % 4]

    z_copies = {}

    def z_send(rel_from, rel_to):
        hop = rel_to - rel_from
        peer = device(x, y, (z - hop) % NZ, core)
        p = position(rel_to)
        z_copies[rel_to] = [
            send(spot(half, position(rel_from)), spot(half, p), zs.at[half, p], zr.at[half, p], peer) for half in (0, 1)
        ]

    def z_wait(*rels):
        for rel in rels:
            for copy in z_copies[rel]:
                copy.wait_recv()

    first_copies, second_copies, sib_copies = {}, {}, {}

    def first(g):
        first_copies[g] = []
        for i in range(3):
            for half, peers in ((0, y_peers), (1, x_peers)):
                ref = c_ref.at[core, half, g, (x, y)[half], (y, x)[half]]
                first_copies[g].append(send(ref, ref, fs.at[half, g, i], fr.at[half, g, i], peers[i]))

    def second(g):
        for copy in first_copies[g]:
            copy.wait_recv()
        second_copies[g] = []
        for i in range(3):
            for half, peers in ((0, x_peers), (1, y_peers)):
                ref = c_ref.at[core, half, g, (x, y)[half]]
                second_copies[g].append(send(ref, ref, ss.at[half, g, i], sr.at[half, g, i], peers[i]))

    def share(g):
        for copy in second_copies[g]:
            copy.wait_recv()
        sib_copies[g] = []
        for half in (0, 1):
            ref = c_ref.at[core, half, g]
            sib_copies[g].append(send(ref, ref, ks.at[half, g], kr.at[half, g], sibling))

    own[0].wait()
    own[1].wait()
    for rel in (2, -2, 1, -1):
        z_send(0, rel)

    row_copies = []
    for i, (dx, dy) in enumerate([(dx, dy) for dx in range(NX) for dy in (0, 1) if dx or dy]):
        px, py = (x + dx) % NX, (y_twin if dy else y)
        ptm = (py % 2) * NX + px
        src = rows_hbm.at[pl.ds(pl.multiple_of(ptm * 64, 64), 64)]
        row_copies.append(send(src, r_ref.at[tm], rs.at[i], rr.at[i], device(px, py, z, core)))

    z_wait(2)
    z_send(2, 4)
    z_send(2, 3)
    z_wait(-2)
    z_send(-2, -4)
    z_send(-2, -3)
    z_wait(1, -1)
    first(0)
    z_wait(4)
    z_send(4, 6)
    z_send(4, 5)
    z_wait(-4)
    z_send(-4, -6)
    z_send(-4, -5)
    z_wait(3, -3)
    first(1)
    second(0)
    z_wait(6)
    z_send(6, 8)
    z_send(6, 7)
    z_wait(-6)
    z_send(-6, -7)
    z_wait(5, -5)
    first(2)
    second(1)
    share(0)
    z_wait(8, 7, -7)
    first(3)
    second(2)
    share(1)
    second(3)
    share(2)
    share(3)
    own[2].wait()
    for copy in row_copies:
        copy.wait_recv()
    for g in range(4):
        for copy in sib_copies[g]:
            copy.wait_recv()
    for copy in started:
        copy.wait_send()


def compute_kernel(c_ref, r_ref, occ_ref, order_ref, levels_ref, times_ref, quad_ref, freqs_ref, o_ref, s_ref, w_ref, k_ref):
    step = pl.program_id(0)
    z = here()[2]

    @pl.when(step == 0)
    def _():
        order = order_ref[...]
        low, high = order % 128, order // 128
        n = order.shape[1]
        lanes = (lax.broadcasted_iota(jnp.int32, (128, n), 0) == low).astype(jnp.float32)
        picked = jnp.dot(
            levels_ref[...], lanes, precision=lax.Precision.HIGHEST, preferred_element_type=jnp.float32
        )
        mine = lax.broadcasted_iota(jnp.int32, picked.shape, 0) == high
        energy = jnp.sum(jnp.where(mine, picked, 0.0), axis=0, keepdims=True)
        filled = occ_ref[...].astype(jnp.float32) * 0.5
        for j in range(8):
            decay = jnp.exp(-times_ref[j] * energy)
            for which, share in ((0, filled), (1, 1.0 - filled)):
                weight = share * decay
                base = (which * 8 + j) * 64
                for t in range(8):
                    rows = r_ref[t].astype(jnp.float32)
                    s_ref[pl.ds(base, 64), pl.ds(t * 256, 256)] = (rows * weight[:, t * 256 : (t + 1) * 256]).astype(
                        jnp.bfloat16
                    )
        angle = jnp.zeros((8, 128), jnp.float32)
        row = lax.broadcasted_iota(jnp.int32, (8, 128), 0)
        lane = lax.broadcasted_iota(jnp.int32, (8, 128), 1)
        quad = jnp.zeros((8, 128), jnp.float32)
        for i in range(8):
            angle = jnp.where(row == i, freqs_ref[i], angle)
        times = jnp.zeros((8, 128), jnp.float32)
        for i in range(8):
            times = jnp.where(lane == i, times_ref[i], times)
            quad = jnp.where(lane == i, quad_ref[i], quad)
        cosines = quad * jnp.cos(angle * times)
        for k in range(8):
            for j in range(8):
                k_ref[k * 8 + j] = jnp.broadcast_to(cosines[k : k + 1, j : j + 1], (8, 128))

    y_hi, pair = step // 2, step % 2
    for i in range(8):
        rel = lax.rem(pair * 8 + i - z + 2 * NZ, NZ)
        pos = jnp.where(rel <= 8, jnp.maximum(2 * rel - 1, 0), 2 * (NZ - rel))
        g, slot = pos // 4, pos % 4
        for core in range(2):
            at = pl.ds(i * 32 + core * 16, 16)
            for t in range(8):
                y_lo, x = t // 4, t % 4
                y = y_hi * 2 + y_lo
                w_ref[at, pl.ds(t * 256, 128)] = c_ref[core, 0, g, x, y, slot]
                w_ref[at, pl.ds(t * 256 + 128, 128)] = c_ref[core, 1, g, y, x, slot]
    greens = lax.dot_general(
        s_ref[...], w_ref[...], (((1,), (1,)), ((), ())), preferred_element_type=jnp.float32
    )
    polar = (greens[:512] * greens[512:]).astype(jnp.bfloat16).astype(jnp.float32)
    for rt in range(8):
        for lt in range(2):
            parts = [polar[j * 64 + rt * 8 : j * 64 + rt * 8 + 8, lt * 128 : lt * 128 + 128] for j in range(8)]
            for k in range(8):
                total = k_ref[k * 8] * parts[0]
                for j in range(1, 8):
                    total = total + k_ref[k * 8 + j] * parts[j]
                o_ref[k, pl.ds(rt * 8, 8), pl.ds(lt * 128, 128)] = total


def body(row_orbitals, column_orbitals, occupation, order, levels, times, quad_weights, freqs):
    any_spec = pl.BlockSpec(memory_space=pl.ANY)
    vmem = pl.BlockSpec(memory_space=pltpu.VMEM)
    smem = pl.BlockSpec(memory_space=pltpu.SMEM)
    dma = pltpu.SemaphoreType.DMA
    columns, rows = pl.pallas_call(
        gather_kernel,
        out_shape=(
            pltpu.VMEM((2, 2, 4, 4, 4, 4, 16, 128), jnp.bfloat16),
            pltpu.VMEM((8, 64, 256), jnp.bfloat16),
        ),
        in_specs=[any_spec, any_spec],
        out_specs=(vmem, vmem),
        scratch_shapes=[
            dma((2, 16)), dma((2, 16)), dma((7,)), dma((7,)), dma((2, 4, 3)), dma((2, 4, 3)),
            dma((2, 4, 3)), dma((2, 4, 3)), dma((2, 4)), dma((2, 4)), dma((3,)),
        ],
        compiler_params=pltpu.CompilerParams(collective_id=0, has_side_effects=True, vmem_limit_bytes=16 * 2**20),
        name="gather",
    )(row_orbitals, column_orbitals)

    count = order.shape[0]
    return pl.pallas_call(
        compute_kernel,
        grid=(4,),
        out_shape=jax.ShapeDtypeStruct((8, 64, 1024), jnp.float32),
        in_specs=[vmem, vmem, vmem, vmem, vmem, smem, smem, smem],
        out_specs=pl.BlockSpec((8, 64, 256), lambda i: (0, 0, i)),
        scratch_shapes=[
            pltpu.VMEM((1024, 2048), jnp.bfloat16),
            pltpu.VMEM((256, 2048), jnp.bfloat16),
            pltpu.VMEM((64, 8, 128), jnp.float32),
        ],
        compiler_params=pltpu.CompilerParams(vmem_limit_bytes=40 * 2**20),
        name="compute",
    )(
        columns, rows, occupation.reshape(1, count), order.reshape(1, count), levels.reshape(count // 128, 128),
        times, quad_weights, freqs,
    )


def solution(mesh):
    placed = (P("space", "tm"), P("space", "tm"), P(), P(), P(), P(), P(), P())
    return jax.shard_map(
        body, mesh=mesh, in_specs=placed, out_specs=P(None, ("space", "tm"), None), check_vma=False
    )
```

time: 139 us -> 58.4 us (0.42)
  the two profiles are of different devices: /device:TPU:12 before, /device:TPU:1 now
where the time goes in v1:
time: 58.4 us; the launch traced here: 58 us
  Pallas kernels  52.3 us (90%)
  local copies, waits for them, and re-layouts  5.69 us (10%)
    pallas_call x1, Pallas kernels, body(): pl.pallas_call(gather_kernel, out_shape=(pltpu.VMEM((2, 2, 4, 4, 4, 4, 16...  41.5 us
    pallas_call x1, Pallas kernels, body(): pl.pallas_call(compute_kernel, grid=(4,), out_shape=jax.ShapeDtypeStruct(...  10.7 us
    unnamed x16, local copies, waits for them, and re-layouts  5.69 us

profile of v1, /device:TPU:1, one launch (start us, length us, event | category | flops | bytes accessed | tf_op | source)
XLA Modules:
  0.0 58.0 jit_solution(2350821782354151527)
XLA Ops:
  0.0 0.0 copy-start
  0.0 0.9 %copy-done = bf16[512,256]{1,0:T(8,128)(2,1)S(1)} copy-done((bf16[512,256]{1,0:T(8,128)(2,1)S(1)}, bf16[512,256]{1,0:T(8,128)(2,1)}, u32[]{:S(2)}) %copy-start) | copy-done | bytes 262168
  1.0 0.0 copy-start.4
  1.0 0.7 %copy-done.4 = bf16[16,256]{1,0:T(8,128)(2,1)S(1)} copy-done((bf16[16,256]{1,0:T(8,128)(2,1)S(1)}, bf16[16,256]{1,0:T(8,128)(2,1)}, u32[]{:S(2)}) %copy-start.4) | copy-done | bytes 8216
  1.6 41.5 %gather.1 = (bf16[2,2,4,4,4,4,16,128]{7,6,5,4,3,2,1,0:T(8,128)(2,1)S(1)}, bf16[8,64,256]{2,1,0:T(8,128)(2,1)S(1)}) custom-call(bf16[512,256]{1,0:T(8,128)(2,1)S(1)} %copy-done, bf16[16,256]{1,0:T(8,128)(2,1)S(1)} %copy-done.4), custom_call_target="tpu_custom_call" | custom-call | tf_op jit(solution)/shard_map/gather/pallas_call | solution.py:234
  43.2 0.0 copy-start.1
  43.2 0.7 %copy-done.1 = s32[2048]{0:T(1024)S(1)} copy-done((s32[2048]{0:T(1024)S(1)}, s32[2048]{0:T(1024)}, u32[]{:S(2)}) %copy-start.1) | copy-done | bytes 8216
  43.9 0.0 copy-start.2
  43.9 0.7 %copy-done.2 = s32[2048]{0:T(1024)S(1)} copy-done((s32[2048]{0:T(1024)S(1)}, s32[2048]{0:T(1024)}, u32[]{:S(2)}) %copy-start.2) | copy-done | bytes 8216
  44.6 0.0 copy-start.3
  44.6 0.7 %copy-done.3 = f32[2048]{0:T(1024)S(1)} copy-done((f32[2048]{0:T(1024)S(1)}, f32[2048]{0:T(1024)}, u32[]{:S(2)}) %copy-start.3) | copy-done | bytes 8216
  45.3 0.0 copy-start.5
  45.3 0.7 %copy-done.5 = f32[8]{0:T(128)S(1)} copy-done((f32[8]{0:T(128)S(1)}, f32[8]{0:T(128)}, u32[]{:S(2)}) %copy-start.5) | copy-done | bytes 56
  45.9 0.0 copy-start.6
  45.9 0.7 %copy-done.6 = f32[8]{0:T(128)S(1)} copy-done((f32[8]{0:T(128)S(1)}, f32[8]{0:T(128)}, u32[]{:S(2)}) %copy-start.6) | copy-done | bytes 56
  46.6 0.0 copy-start.7
  46.6 0.7 %copy-done.7 = f32[8]{0:T(128)S(1)} copy-done((f32[8]{0:T(128)S(1)}, f32[8]{0:T(128)}, u32[]{:S(2)}) %copy-start.7) | copy-done | bytes 56
  47.2 10.7 %compute.1 = f32[8,64,1024]{2,1,0:T(8,128)} custom-call(bf16[2,2,4,4,4,4,16,128]{7,6,5,4,3,2,1,0:T(8,128)(2,1)S(1)} %get-tuple-element.7.c_ref, bf16[8,64,256]{2,1,0:T(8,128)(2,1)S(1)} %get-tuple-element.8.r_ref, s32[1,2048]{1,0:T(1,128)S(1)} %bitcast.3, s32[1,2048]{1,0:T(1,128)S(1)} %bitcast.4, f32[16,128]{1,0:T(8,128)S(1)} %bitcast.5, f32[8]{0:T(128)S(1)} %copy-done.5, ...), custom_call_target="tpu_custom_call" | custom-call | tf_op jit(solution)/shard_map/compute/pallas_call | solution.py:251
Async XLA Ops:
  0.0 0.9 %copy-start = (bf16[512,256]{1,0:T(8,128)(2,1)S(1)}, bf16[512,256]{1,0:T(8,128)(2,1)}, u32[]{:S(2)}) copy-start(bf16[512,256]{1,0:T(8,128)(2,1)} %rows_hbm.1) | copy-start | bytes 786436
  1.0 0.7 %copy-start.4 = (bf16[16,256]{1,0:T(8,128)(2,1)S(1)}, bf16[16,256]{1,0:T(8,128)(2,1)}, u32[]{:S(2)}) copy-start(bf16[16,256]{1,0:T(8,128)(2,1)} %columns_hbm.1) | copy-start | bytes 24580
  43.2 0.7 %copy-start.1 = (s32[2048]{0:T(1024)S(1)}, s32[2048]{0:T(1024)}, u32[]{:S(2)}) copy-start(s32[2048]{0:T(1024)} %param.10) | copy-start | bytes 24580
  43.9 0.7 %copy-start.2 = (s32[2048]{0:T(1024)S(1)}, s32[2048]{0:T(1024)}, u32[]{:S(2)}) copy-start(s32[2048]{0:T(1024)} %param.11) | copy-start | bytes 24580
  44.6 0.7 %copy-start.3 = (f32[2048]{0:T(1024)S(1)}, f32[2048]{0:T(1024)}, u32[]{:S(2)}) copy-start(f32[2048]{0:T(1024)} %param.12) | copy-start | bytes 24580
  45.3 0.7 %copy-start.5 = (f32[8]{0:T(128)S(1)}, f32[8]{0:T(128)}, u32[]{:S(2)}) copy-start(f32[8]{0:T(128)} %times_ref.1) | copy-start | bytes 100
  45.9 0.7 %copy-start.6 = (f32[8]{0:T(128)S(1)}, f32[8]{0:T(128)}, u32[]{:S(2)}) copy-start(f32[8]{0:T(128)} %quad_ref.1) | copy-start | bytes 100
  46.6 0.7 %copy-start.7 = (f32[8]{0:T(128)S(1)}, f32[8]{0:T(128)}, u32[]{:S(2)}) copy-start(f32[8]{0:T(128)} %freqs_ref.1) | copy-start | bytes 100

commit v2 on v1

v2 whole, which is shorter than its diff:
```python
import functools

import jax
import jax.numpy as jnp
from jax import lax
from jax.experimental import pallas as pl
from jax.experimental.pallas import tpu as pltpu
from jax.sharding import PartitionSpec as P

MESH = pl.DeviceIdType.MESH
NX, NY, NZ = 4, 4, 16


def here():
    space, tm = lax.axis_index("space"), lax.axis_index("tm")
    y = lax.div(space, 32) * 2 + lax.div(tm, NX)
    return lax.rem(tm, NX), y, lax.rem(lax.div(space, 2), NZ), lax.rem(space, 2)


def device(x, y, z, core):
    return ((lax.div(y, 2) * NZ + z) * 2 + core, lax.rem(y, 2) * NX + x)


def position(rel):
    return 2 * rel - 1 if rel > 0 else -2 * rel


def gather_kernel(
    rows_hbm, columns_hbm, occ_hbm, order_hbm, levels_hbm, times_hbm, quad_hbm, freqs_hbm,
    c_ref, s_ref, k_ref,
    r_ref, occ_ref, order_ref, levels_ref, decay_ref, times_ref, quad_ref, freqs_ref,
    zs, zr, rs, rr, fs, fr, ss, sr, ks, kr, local,
):
    x, y, z, core = here()
    tm = lax.axis_index("tm")

    own = [
        pltpu.make_async_copy(src, dst, local.at[i])
        for i, (src, dst) in enumerate([
            (columns_hbm.at[:, pl.ds(0, 128)], c_ref.at[core, 0, 0, x, y, 0]),
            (columns_hbm.at[:, pl.ds(128, 128)], c_ref.at[core, 1, 0, y, x, 0]),
            (rows_hbm.at[pl.ds(pl.multiple_of(tm * 64, 64), 64)], r_ref.at[tm]),
            (occ_hbm, occ_ref),
            (order_hbm, order_ref),
            (levels_hbm, levels_ref),
            (times_hbm, times_ref),
            (quad_hbm, quad_ref),
            (freqs_hbm, freqs_ref),
        ])
    ]
    for copy in own:
        copy.start()

    z_peers = [device(x, y, lax.rem(z + d, NZ), core) for d in (4, 12, 3, 13, 2, 14, 1, 15)]
    x_peers = [device(lax.rem(x + d, NX), y, z, core) for d in (2, 1, 3)]
    y_peers = [device(x, lax.rem(y + d, NY), z, core) for d in (2, 1, 3)]
    y_twin = y + 1 - 2 * lax.rem(y, 2)
    diagonal = [device(lax.rem(x + dx, NX), y_twin, z, core) for dx in range(1, NX)]
    sibling = device(x, y, z, 1 - core)

    barrier = pltpu.get_barrier_semaphore()
    greeted = z_peers + x_peers + y_peers + diagonal + [sibling]
    for peer in greeted:
        pl.semaphore_signal(barrier, inc=1, device_id=peer, device_id_type=MESH)
    pl.semaphore_wait(barrier, len(greeted))

    started = []

    def send(src, dst, send_sem, recv_sem, peer):
        copy = pltpu.make_async_remote_copy(
            src_ref=src, dst_ref=dst, send_sem=send_sem, recv_sem=recv_sem, device_id=peer, device_id_type=MESH
        )
        copy.start()
        started.append(copy)
        return copy

    def spot(half, p):
        return c_ref.at[core, half, p // 4, (x, y)[half], (y, x)[half], p % 4]

    z_copies = {}

    def z_send(rel_from, rel_to):
        hop = rel_to - rel_from
        peer = device(x, y, lax.rem(z - hop + NZ, NZ), core)
        p = position(rel_to)
        z_copies[rel_to] = [
            send(spot(half, position(rel_from)), spot(half, p), zs.at[half, p], zr.at[half, p], peer) for half in (0, 1)
        ]

    def z_wait(*rels):
        for rel in rels:
            for copy in z_copies[rel]:
                copy.wait_recv()

    first_copies, second_copies, sib_copies = {}, {}, {}

    def first(g):
        first_copies[g] = []
        for i in range(3):
            for half, peers in ((0, y_peers), (1, x_peers)):
                ref = c_ref.at[core, half, g, (x, y)[half], (y, x)[half]]
                first_copies[g].append(send(ref, ref, fs.at[half, g, i], fr.at[half, g, i], peers[i]))

    def second(g):
        for copy in first_copies[g]:
            copy.wait_recv()
        second_copies[g] = []
        for i in range(3):
            for half, peers in ((0, x_peers), (1, y_peers)):
                ref = c_ref.at[core, half, g, (x, y)[half]]
                second_copies[g].append(send(ref, ref, ss.at[half, g, i], sr.at[half, g, i], peers[i]))

    def share(g):
        for copy in second_copies[g]:
            copy.wait_recv()
        sib_copies[g] = []
        for half in (0, 1):
            ref = c_ref.at[core, half, g]
            sib_copies[g].append(send(ref, ref, ks.at[half, g], kr.at[half, g], sibling))

    own[0].wait()
    own[1].wait()
    for rel in (4, -4, 2, -2, 1, -1, 3, -3):
        z_send(0, rel)

    row_copies = []
    for i, (dx, dy) in enumerate([(dx, dy) for dy in (1, 0) for dx in (2, 1, 3, 0) if dx or dy]):
        px, py = lax.rem(x + dx, NX), (y_twin if dy else y)
        ptm = lax.rem(py, 2) * NX + px
        src = rows_hbm.at[pl.ds(pl.multiple_of(ptm * 64, 64), 64)]
        row_copies.append(send(src, r_ref.at[tm], rs.at[i], rr.at[i], device(px, py, z, core)))

    for copy in own[2:]:
        copy.wait()
    order = order_ref[...]
    low, high = lax.rem(order, 128), lax.div(order, 128)
    n = order.shape[1]
    chosen = (lax.broadcasted_iota(jnp.int32, (128, n), 0) == low).astype(jnp.float32)
    picked = jnp.dot(levels_ref[...], chosen, precision=lax.Precision.HIGHEST, preferred_element_type=jnp.float32)
    mine = lax.broadcasted_iota(jnp.int32, picked.shape, 0) == high
    energy = jnp.sum(jnp.where(mine, picked, 0.0), axis=0, keepdims=True)
    row8 = lax.broadcasted_iota(jnp.int32, (8, n), 0)
    times8 = jnp.zeros((8, n), jnp.float32)
    for j in range(8):
        times8 = jnp.where(row8 == j, times_ref[j], times8)
    decays = jnp.exp(-times8 * energy)
    filled = occ_ref[...].astype(jnp.float32) * 0.5
    decay_ref[0] = filled * decays
    decay_ref[1] = (1.0 - filled) * decays

    row = lax.broadcasted_iota(jnp.int32, (8, 128), 0)
    lane = lax.broadcasted_iota(jnp.int32, (8, 128), 1)
    zero = jnp.zeros((8, 128), jnp.float32)
    freq, time, quad = zero, zero, zero
    for i in range(8):
        freq = jnp.where(row == i, freqs_ref[i], freq)
        time = jnp.where(lane == i, times_ref[i], time)
        quad = jnp.where(lane == i, quad_ref[i], quad)
    cosines = quad * jnp.cos(freq * time)
    for k in range(8):
        for j in range(8):
            k_ref[k * 8 + j] = jnp.broadcast_to(cosines[k : k + 1, j : j + 1], (8, 128))

    def scale(which):
        for t in range(8):
            rows = r_ref[t].astype(jnp.float32)
            for j in range(8):
                weight = decay_ref[which, j : j + 1, t * 256 : (t + 1) * 256]
                s_ref[pl.ds((which * 8 + j) * 64, 64), pl.ds(t * 256, 256)] = (rows * weight).astype(jnp.bfloat16)

    z_wait(1, -1, 2)
    first(0)
    z_wait(4, -4)
    for rel in (8, 6, 5, 7):
        z_send(4, rel)
        if rel < 8:
            z_send(-4, -rel)
    z_wait(-2, 3, -3)
    first(1)
    for copy in row_copies:
        copy.wait_recv()
    scale(0)
    second(0)
    z_wait(5, -5, 6)
    first(2)
    second(1)
    z_wait(-6, 7, -7, 8)
    first(3)
    share(0)
    scale(1)
    share(1)
    second(2)
    second(3)
    share(2)
    share(3)
    for g in range(4):
        for copy in sib_copies[g]:
            copy.wait_recv()
    for copy in started:
        copy.wait_send()


def compute_kernel(c_ref, s_ref, k_ref, o_ref, w_ref):
    step = pl.program_id(0)
    z = here()[2]
    y_hi, pair = lax.div(step, 2), lax.rem(step, 2)
    for i in range(8):
        rel = lax.rem(pair * 8 + i - z + 2 * NZ, NZ)
        pos = jnp.where(rel <= 8, jnp.maximum(2 * rel - 1, 0), 2 * (NZ - rel))
        g, slot = lax.div(pos, 4), lax.rem(pos, 4)
        for core in range(2):
            at = pl.ds(i * 32 + core * 16, 16)
            for t in range(8):
                y_lo, x = t // 4, t % 4
                y = y_hi * 2 + y_lo
                w_ref[at, pl.ds(t * 256, 128)] = c_ref[core, 0, g, x, y, slot]
                w_ref[at, pl.ds(t * 256 + 128, 128)] = c_ref[core, 1, g, y, x, slot]
    greens = lax.dot_general(
        s_ref[...], w_ref[...], (((1,), (1,)), ((), ())), preferred_element_type=jnp.float32
    )
    polar = (greens[:512] * greens[512:]).astype(jnp.bfloat16).astype(jnp.float32)
    for rt in range(8):
        for lt in range(2):
            parts = [polar[j * 64 + rt * 8 : j * 64 + rt * 8 + 8, lt * 128 : lt * 128 + 128] for j in range(8)]
            for k in range(8):
                total = k_ref[k * 8] * parts[0]
                for j in range(1, 8):
                    total = total + k_ref[k * 8 + j] * parts[j]
                o_ref[k, pl.ds(rt * 8, 8), pl.ds(lt * 128, 128)] = total


def body(row_orbitals, column_orbitals, occupation, order, levels, times, quad_weights, freqs):
    hbm = pl.BlockSpec(memory_space=pltpu.HBM)
    vmem = pl.BlockSpec(memory_space=pltpu.VMEM)
    dma = pltpu.SemaphoreType.DMA
    count = order.shape[0]
    columns, scaled, cosines = pl.pallas_call(
        gather_kernel,
        out_shape=(
            pltpu.VMEM((2, 2, 4, 4, 4, 4, 16, 128), jnp.bfloat16),
            pltpu.VMEM((1024, 2048), jnp.bfloat16),
            pltpu.VMEM((64, 8, 128), jnp.float32),
        ),
        in_specs=[hbm] * 8,
        out_specs=(vmem, vmem, vmem),
        scratch_shapes=[
            pltpu.VMEM((8, 64, 256), jnp.bfloat16),
            pltpu.VMEM((1, count), jnp.int32),
            pltpu.VMEM((1, count), jnp.int32),
            pltpu.VMEM((count // 128, 128), jnp.float32),
            pltpu.VMEM((2, 8, count), jnp.float32),
            pltpu.SMEM((8,), jnp.float32),
            pltpu.SMEM((8,), jnp.float32),
            pltpu.SMEM((8,), jnp.float32),
            dma((2, 16)), dma((2, 16)), dma((7,)), dma((7,)), dma((2, 4, 3)), dma((2, 4, 3)),
            dma((2, 4, 3)), dma((2, 4, 3)), dma((2, 4)), dma((2, 4)), dma((9,)),
        ],
        compiler_params=pltpu.CompilerParams(collective_id=0, has_side_effects=True, vmem_limit_bytes=58384384),
        name="gather",
    )(
        row_orbitals, column_orbitals, occupation.reshape(1, count), order.reshape(1, count),
        levels.reshape(count // 128, 128), times, quad_weights, freqs,
    )
    return pl.pallas_call(
        compute_kernel,
        grid=(4,),
        out_shape=jax.ShapeDtypeStruct((8, 64, 1024), jnp.float32),
        in_specs=[vmem, vmem, vmem],
        out_specs=pl.BlockSpec((8, 64, 256), lambda i: (0, 0, i)),
        scratch_shapes=[pltpu.VMEM((256, 2048), jnp.bfloat16)],
        compiler_params=pltpu.CompilerParams(vmem_limit_bytes=40 * 2**20),
        name="compute",
    )(columns, scaled, cosines)


def solution(mesh):
    placed = (P("space", "tm"), P("space", "tm"), P(), P(), P(), P(), P(), P())
    return jax.shard_map(
        body, mesh=mesh, in_specs=placed, out_specs=P(None, ("space", "tm"), None), check_vma=False
    )
```

time: 58.4 us -> 48 us (0.82)
  local copies, waits for them, and re-layouts: 5.69 us -> 0 us
  Pallas kernels: 52.3 us -> 47.9 us
    unnamed x16 -> x0, local copies, waits for them, and re-layouts: 5.69 us -> none
    pallas_call x1, Pallas kernels: 10.7 us -> 7.65 us  [body(): pl.pallas_call(compute_kernel, grid=(4,), out_shape=jax.ShapeDtypeStruct(...]
    pallas_call x1, Pallas kernels: 41.5 us -> 40.2 us  [body(): pl.pallas_call(gather_kernel, out_shape=(pltpu.VMEM((2, 2, 4, 4, 4, 4, 16...]
where the time goes in v2:
time: 48 us; the launch traced here: 47.9 us
  Pallas kernels  47.9 us (100%)
    pallas_call x1, Pallas kernels, body(): pl.pallas_call(gather_kernel, out_shape=(pltpu.VMEM((2, 2, 4, 4, 4, 4, 16...  40.2 us
    pallas_call x1, Pallas kernels, body(): pl.pallas_call(compute_kernel, grid=(4,), out_shape=jax.ShapeDtypeStruct(...  7.65 us

profile of v2, /device:TPU:1, one launch (start us, length us, event | category | flops | bytes accessed | tf_op | source)
XLA Modules:
  0.0 47.9 jit_solution(11894055814460433979)
XLA Ops:
  0.0 40.2 %gather.1 = (bf16[2,2,4,4,4,4,16,128]{7,6,5,4,3,2,1,0:T(8,128)(2,1)S(1)}, bf16[1024,2048]{1,0:T(8,128)(2,1)S(1)}, f32[64,8,128]{2,1,0:T(8,128)S(1)}) custom-call(bf16[512,256]{1,0:T(8,128)(2,1)} %rows_hbm.1, bf16[16,256]{1,0:T(8,128)(2,1)} %columns_hbm.1, s32[1,2048]{1,0:T(1,128)} %bitcast.3, s32[1,2048]{1,0:T(1,128)} %bitcast.4, f32[16,128]{1,0:T(8,128)} %bitcast.5, ...), custom_call_target="tpu_custom_call" | custom-call | tf_op jit(solution)/shard_map/gather/pallas_call | solution.py:237
  40.3 7.6 %compute.1 = f32[8,64,1024]{2,1,0:T(8,128)} custom-call(bf16[2,2,4,4,4,4,16,128]{7,6,5,4,3,2,1,0:T(8,128)(2,1)S(1)} %get-tuple-element.8.c_ref, bf16[1024,2048]{1,0:T(8,128)(2,1)S(1)} %get-tuple-element.9.s_ref, f32[64,8,128]{2,1,0:T(8,128)S(1)} %get-tuple-element.10.k_ref), custom_call_target="tpu_custom_call" | custom-call | tf_op jit(solution)/shard_map/compute/pallas_call | solution.py:264

commit v3 on v2

v3 whole, which is shorter than its diff:
```python
import functools

import jax
import jax.numpy as jnp
from jax import lax
from jax.experimental import pallas as pl
from jax.experimental.pallas import tpu as pltpu
from jax.sharding import PartitionSpec as P

MESH = pl.DeviceIdType.MESH
NX, NY, NZ = 4, 4, 16


def here():
    space, tm = lax.axis_index("space"), lax.axis_index("tm")
    y = lax.div(space, 32) * 2 + lax.div(tm, NX)
    return lax.rem(tm, NX), y, lax.rem(lax.div(space, 2), NZ), lax.rem(space, 2)


def device(x, y, z, core):
    return ((lax.div(y, 2) * NZ + z) * 2 + core, lax.rem(y, 2) * NX + x)


NEAR = {0: 0, 1: 1, -1: 2}
FAR = {
    2: (0, 0), -2: (0, 1), 3: (0, 2), -3: (0, 3), 4: (0, 4), -4: (0, 5),
    5: (1, 0), -5: (1, 1), 6: (1, 2), -6: (1, 3), 7: (1, 4), -7: (1, 5), 8: (1, 6),
}
WIDTH = (6, 7)
BASE = (48, 144)
HALF = 256


EARLY = (1, -1, 2, -2, 3, -3, 4, -4)
LATE = (5, -5, 6, -6, 7, -7, 8, 0)


def polar_of(planes, core, c_ref, s_ref, w_ref):
    for i, (y_hi, rel) in enumerate([(y_hi, rel) for y_hi in range(2) for rel in planes]):
        start, width = (NEAR[rel] * 16, 1) if rel in NEAR else (BASE[FAR[rel][0]] + FAR[rel][1], WIDTH[FAR[rel][0]])
        at = pl.ds(i * 16, 16)
        for t in range(8):
            x, y = t % 4, y_hi * 2 + t // 4
            w_ref[at, pl.ds(t * 256, 128)] = c_ref[core * 2 * HALF + start + (x * 4 + y) * width]
            w_ref[at, pl.ds(t * 256 + 128, 128)] = c_ref[(core * 2 + 1) * HALF + start + (y * 4 + x) * width]
    full, empty = (
        lax.dot_general(
            s_ref[pl.ds(which * 512, 512)], w_ref[...], (((1,), (1,)), ((), ())), preferred_element_type=jnp.float32
        )
        for which in range(2)
    )
    return (full * empty).astype(jnp.bfloat16)


def gather_kernel(
    rows_hbm, columns_hbm, occ_hbm, order_hbm, levels_hbm, times_hbm, quad_hbm, freqs_hbm,
    c_ref, s_ref, k_ref, p_ref, q_ref,
    w_ref, r_ref, occ_ref, order_ref, levels_ref, decay_ref, times_ref, quad_ref, freqs_ref,
    zs, zr, rs, rr, fs, fr, ss, sr, ps, pr, ks, kr, local,
):
    x, y, z, core = here()
    tm = lax.axis_index("tm")

    ab = (x * 4 + y, y * 4 + x)
    lead = (x, y)

    def tiles(half, start, count):
        return c_ref.at[pl.ds((core * 2 + half) * HALF + start, count)]

    def near(half, rel, first, count):
        return tiles(half, NEAR[rel] * 16 + first, count)

    def far(half, group, first, count):
        return tiles(half, BASE[group] + first * WIDTH[group], count * WIDTH[group])

    def far_one(half, rel):
        group, slot = FAR[rel]
        return tiles(half, BASE[group] + ab[half] * WIDTH[group] + slot, 1)

    own = [
        pltpu.make_async_copy(src, dst, local.at[i])
        for i, (src, dst) in enumerate([
            (columns_hbm.at[:, pl.ds(0, 128)], c_ref.at[core * 2 * HALF + ab[0]]),
            (columns_hbm.at[:, pl.ds(128, 128)], c_ref.at[(core * 2 + 1) * HALF + ab[1]]),
            (rows_hbm.at[pl.ds(pl.multiple_of(tm * 64, 64), 64)], r_ref.at[tm]),
            (occ_hbm, occ_ref),
            (order_hbm, order_ref),
            (levels_hbm, levels_ref),
            (times_hbm, times_ref),
            (quad_hbm, quad_ref),
            (freqs_hbm, freqs_ref),
        ])
    ]
    own[0].start()
    own[1].start()

    z_peers = [device(x, y, lax.rem(z + d, NZ), core) for d in (4, 12, 3, 13, 2, 14, 1, 15)]
    x_peers = [device(lax.rem(x + d, NX), y, z, core) for d in (2, 1, 3)]
    y_peers = [device(x, lax.rem(y + d, NY), z, core) for d in (2, 1, 3)]
    y_twin = y + 1 - 2 * lax.rem(y, 2)
    diagonal = [device(lax.rem(x + dx, NX), y_twin, z, core) for dx in range(1, NX)]
    sibling = device(x, y, z, 1 - core)

    barrier = pltpu.get_barrier_semaphore()
    greeted = z_peers + x_peers + y_peers + diagonal + [sibling]
    for peer in greeted:
        pl.semaphore_signal(barrier, inc=1, device_id=peer, device_id_type=MESH)
    for copy in own[2:]:
        copy.start()
    pl.semaphore_wait(barrier, len(greeted))

    started = []

    def send(src, dst, send_sem, recv_sem, peer):
        copy = pltpu.make_async_remote_copy(
            src_ref=src, dst_ref=dst, send_sem=send_sem, recv_sem=recv_sem, device_id=peer, device_id_type=MESH
        )
        copy.start()
        started.append(copy)
        return copy

    def wait(copies):
        for copy in copies:
            copy.wait_recv()

    z_copies = {}

    def z_send(rel_from, rel_to):
        peer = device(x, y, lax.rem(z - (rel_to - rel_from) + NZ, NZ), core)
        group, slot = FAR[rel_to]
        at = group * 6 + slot
        z_copies[rel_to] = [
            send(
                near(half, 0, ab[half], 1) if rel_from == 0 else far_one(half, rel_from),
                far_one(half, rel_to), zs.at[half, at], zr.at[half, at], peer,
            )
            for half in (0, 1)
        ]

    def spread(refs, peers, send_sems, recv_sems):
        return [
            send(refs[half], refs[half], send_sems.at[half, i], recv_sems.at[half, i], peers[half][i])
            for i in range(3)
            for half in (0, 1)
        ]

    def first(group):
        refs = [far(half, group, ab[half], 1) for half in (0, 1)]
        return spread(refs, (y_peers, x_peers), fs.at[group], fr.at[group])

    def second(group):
        refs = [far(half, group, lead[half] * 4, 4) for half in (0, 1)]
        return spread(refs, (x_peers, y_peers), ss.at[group], sr.at[group])

    def share(at, refs):
        return [send(refs[half], refs[half], ks.at[at, half], kr.at[at, half], sibling) for half in (0, 1)]

    own[0].wait()
    own[1].wait()
    for rel in (4, -4, 3, -3, 2, -2):
        z_send(0, rel)
    own_first = spread([near(half, 0, ab[half], 1) for half in (0, 1)], (y_peers, x_peers), fs.at[2], fr.at[2])

    row_copies = []
    for i, (dx, dy) in enumerate([(dx, dy) for dy in (1, 0) for dx in (2, 1, 3, 0) if dx or dy]):
        px, py = lax.rem(x + dx, NX), (y_twin if dy else y)
        ptm = lax.rem(py, 2) * NX + px
        src = rows_hbm.at[pl.ds(pl.multiple_of(ptm * 64, 64), 64)]
        row_copies.append(send(src, r_ref.at[tm], rs.at[i], rr.at[i], device(px, py, z, core)))

    for copy in own[2:]:
        copy.wait()
    order = order_ref[...]
    low, high = lax.rem(order, 128), lax.div(order, 128)
    n = order.shape[1]
    chosen = (lax.broadcasted_iota(jnp.int32, (128, n), 0) == low).astype(jnp.float32)
    picked = jnp.dot(levels_ref[...], chosen, precision=lax.Precision.HIGHEST, preferred_element_type=jnp.float32)
    mine = lax.broadcasted_iota(jnp.int32, picked.shape, 0) == high
    energy = jnp.sum(jnp.where(mine, picked, 0.0), axis=0, keepdims=True)
    row8 = lax.broadcasted_iota(jnp.int32, (8, n), 0)
    times8 = jnp.zeros((8, n), jnp.float32)
    for j in range(8):
        times8 = jnp.where(row8 == j, times_ref[j], times8)
    decays = jnp.exp(-times8 * energy)
    filled = occ_ref[...].astype(jnp.float32) * 0.5
    decay_ref[0] = filled * decays
    decay_ref[1] = (1.0 - filled) * decays

    row = lax.broadcasted_iota(jnp.int32, (8, 128), 0)
    lane = lax.broadcasted_iota(jnp.int32, (8, 128), 1)
    zero = jnp.zeros((8, 128), jnp.float32)
    freq, time, quad = zero, zero, zero
    for i in range(8):
        freq = jnp.where(row == i, freqs_ref[i], freq)
        time = jnp.where(lane == i, times_ref[i], time)
        quad = jnp.where(lane == i, quad_ref[i], quad)
    cosines = quad * jnp.cos(freq * time)
    for k in range(8):
        for j in range(8):
            k_ref[k * 8 + j] = jnp.broadcast_to(cosines[k : k + 1, j : j + 1], (8, 128))

    column = lax.broadcasted_iota(jnp.int32, (1, 512), 1)
    ahead = lax.rem(lax.div(column, 32) - z + NZ, NZ)
    place = jnp.where(ahead <= 8, jnp.maximum(2 * ahead - 1, 0), 2 * (NZ - ahead))
    rank, point = lax.rem(place + 15, 16), lax.rem(column, 32)
    other = jnp.where(lax.div(point, 16) == core, 0, 256)
    source = other + jnp.where(rank < 8, 0, 128) + lax.rem(rank, 8) * 16 + lax.rem(point, 16)
    chosen_rows = (lax.broadcasted_iota(jnp.int32, (512, 512), 0) == source).astype(jnp.float32).astype(jnp.bfloat16)
    q_ref[0] = chosen_rows[:, :256]
    q_ref[1] = chosen_rows[:, 256:]

    def scale(which):
        for t in range(8):
            rows = r_ref[t].astype(jnp.float32)
            for j in range(8):
                weight = decay_ref[which, j : j + 1, t * 256 : (t + 1) * 256]
                s_ref[pl.ds((which * 8 + j) * 64, 64), pl.ds(t * 256, 256)] = (rows * weight).astype(jnp.bfloat16)

    for rel in (4, -4):
        wait(z_copies[rel])
    for rel in (8, 6, 5, 7):
        z_send(4, rel)
        if rel < 8:
            z_send(-4, -rel)
    wait(own_first)
    own_second = spread([near(half, 0, lead[half] * 4, 4) for half in (0, 1)], (x_peers, y_peers), ss.at[2], sr.at[2])
    for rel in (2, -2, 3, -3):
        wait(z_copies[rel])
    first_a = first(0)
    wait(row_copies)
    scale(0)
    scale(1)
    wait(own_second)
    plane_copies = {}
    for i, rel in enumerate((1, -1)):
        peer = device(x, y, lax.rem(z - rel + NZ, NZ), core)
        plane_copies[rel] = [
            send(near(half, 0, 0, 16), near(half, rel, 0, 16), ps.at[i, half], pr.at[i, half], peer) for half in (0, 1)
        ]
    shared_own = share(0, [near(half, 0, 0, 16) for half in (0, 1)])
    for rel in (5, -5, 6, -6, 7, -7, 8):
        wait(z_copies[rel])
    first_b = first(1)
    wait(first_a)
    second_a = second(0)
    shared = []
    for i, rel in enumerate((1, -1)):
        wait(plane_copies[rel])
        shared += share(2 + i, [near(half, rel, 0, 16) for half in (0, 1)])
    wait(first_b)
    second_b = second(1)
    wait(second_a)
    shared += share(1, [far(half, 0, 0, 16) for half in (0, 1)])
    shared_b = share(4, [far(half, 1, lead[half] * 4, 4) for half in (0, 1)])
    p_ref[0] = polar_of(EARLY, core, c_ref, s_ref, w_ref.at[0])
    for at, (i, back) in enumerate(((1, 3), (2, 1), (0, 2))):
        wait(second_b[2 * i : 2 * i + 2])
        shared_b += share(5 + at, [far(half, 1, lax.rem(lead[half] + back, 4) * 4, 4) for half in (0, 1)])
    p_ref[1] = polar_of(LATE, core, c_ref, s_ref, w_ref.at[1])
    wait(shared)
    p_ref[2] = polar_of(EARLY, 1 - core, c_ref, s_ref, w_ref.at[0])
    wait(shared_own)
    wait(shared_b)
    for copy in started:
        copy.wait_send()


def compute_kernel(c_ref, s_ref, k_ref, p_ref, q_ref, o_hbm, w_ref, l_ref, o_ref, sem):
    last = polar_of(LATE, 1 - here()[3], c_ref, s_ref, w_ref)
    for y_hi in range(2):
        for group in range(3):
            l_ref[y_hi, :, pl.ds(group * 128, 128)] = p_ref[group, :, pl.ds(y_hi * 128, 128)]
        l_ref[y_hi, :, pl.ds(384, 128)] = last[:, y_hi * 128 : y_hi * 128 + 128]
    copies = []
    for step in range(4):
        y_hi, part = divmod(step, 2)
        polar = jnp.dot(l_ref[y_hi], q_ref[part], preferred_element_type=jnp.float32)
        for rt in range(8):
            for lt in range(2):
                parts = [polar[j * 64 + rt * 8 : j * 64 + rt * 8 + 8, lt * 128 : lt * 128 + 128] for j in range(8)]
                for k in range(8):
                    total = k_ref[k * 8] * parts[0]
                    for j in range(1, 8):
                        total = total + k_ref[k * 8 + j] * parts[j]
                    o_ref[step, k, pl.ds(rt * 8, 8), pl.ds(lt * 128, 128)] = total
        copy = pltpu.make_async_copy(o_ref.at[step], o_hbm.at[:, :, pl.ds(step * 256, 256)], sem.at[step])
        copy.start()
        copies.append(copy)
    for copy in copies:
        copy.wait()


def body(row_orbitals, column_orbitals, occupation, order, levels, times, quad_weights, freqs):
    hbm = pl.BlockSpec(memory_space=pltpu.HBM)
    vmem = pl.BlockSpec(memory_space=pltpu.VMEM)
    dma = pltpu.SemaphoreType.DMA
    count = order.shape[0]
    columns, scaled, cosines, polar, order_back = pl.pallas_call(
        gather_kernel,
        out_shape=(
            pltpu.VMEM((4 * HALF, 16, 128), jnp.bfloat16),
            pltpu.VMEM((1024, 2048), jnp.bfloat16),
            pltpu.VMEM((64, 8, 128), jnp.float32),
            pltpu.VMEM((3, 512, 256), jnp.bfloat16),
            pltpu.VMEM((2, 512, 256), jnp.bfloat16),
        ),
        in_specs=[hbm] * 8,
        out_specs=(vmem,) * 5,
        scratch_shapes=[
            pltpu.VMEM((2, 256, 2048), jnp.bfloat16),
            pltpu.VMEM((8, 64, 256), jnp.bfloat16),
            pltpu.VMEM((1, count), jnp.int32),
            pltpu.VMEM((1, count), jnp.int32),
            pltpu.VMEM((count // 128, 128), jnp.float32),
            pltpu.VMEM((2, 8, count), jnp.float32),
            pltpu.SMEM((8,), jnp.float32),
            pltpu.SMEM((8,), jnp.float32),
            pltpu.SMEM((8,), jnp.float32),
            dma((2, 13)), dma((2, 13)), dma((7,)), dma((7,)), dma((3, 2, 3)), dma((3, 2, 3)), dma((3, 2, 3)), dma((3, 2, 3)),
            dma((2, 2)), dma((2, 2)), dma((8, 2)), dma((8, 2)), dma((9,)),
        ],
        compiler_params=pltpu.CompilerParams(collective_id=0, has_side_effects=True, vmem_limit_bytes=67043328 - 9961472 - 8192),
        name="gather",
    )(
        row_orbitals, column_orbitals, occupation.reshape(1, count), order.reshape(1, count),
        levels.reshape(count // 128, 128), times, quad_weights, freqs,
    )
    return pl.pallas_call(
        compute_kernel,
        out_shape=jax.ShapeDtypeStruct((8, 64, 1024), jnp.float32),
        in_specs=[vmem] * 5,
        out_specs=hbm,
        scratch_shapes=[
            pltpu.VMEM((256, 2048), jnp.bfloat16),
            pltpu.VMEM((2, 512, 512), jnp.bfloat16),
            pltpu.VMEM((4, 8, 64, 256), jnp.float32),
            dma((4,)),
        ],
        compiler_params=pltpu.CompilerParams(vmem_limit_bytes=40 * 2**20),
        name="compute",
    )(columns, scaled, cosines, polar, order_back)


def solution(mesh):
    placed = (P("space", "tm"), P("space", "tm"), P(), P(), P(), P(), P(), P())
    return jax.shard_map(
        body, mesh=mesh, in_specs=placed, out_specs=P(None, ("space", "tm"), None), check_vma=False
    )
```

time: 48 us -> 44.6 us (0.929)
  Pallas kernels: 47.9 us -> 44.5 us
    pallas_call x2, Pallas kernels: 47.9 us -> 44.5 us  [the longest x1 40.4 us: body(): pl.pallas_call(gather_kernel, out_shape=(pltpu.VMEM((4 * HALF, 16, 128),...]
where the time goes in v3:
time: 44.6 us; the launch traced here: 44.5 us
  Pallas kernels  44.5 us (100%)
    pallas_call x1, Pallas kernels, body(): pl.pallas_call(gather_kernel, out_shape=(pltpu.VMEM((4 * HALF, 16, 128),...  40.4 us
    pallas_call x1, Pallas kernels, body(): pl.pallas_call(compute_kernel, out_shape=jax.ShapeDtypeStruct((8, 64, 102...  4.12 us

profile of v3, /device:TPU:1, one launch (start us, length us, event | category | flops | bytes accessed | tf_op | source)
XLA Modules:
  0.0 44.5 jit_solution(11197500144728249977)
XLA Ops:
  0.0 40.4 %gather.1 = (bf16[1024,16,128]{2,1,0:T(8,128)(2,1)S(1)}, bf16[1024,2048]{1,0:T(8,128)(2,1)S(1)}, f32[64,8,128]{2,1,0:T(8,128)S(1)}, bf16[3,512,256]{2,1,0:T(8,128)(2,1)S(1)}, bf16[2,512,256]{2,1,0:T(8,128)(2,1)S(1)}) custom-call(bf16[512,256]{1,0:T(8,128)(2,1)} %rows_hbm.1, bf16[16,256]{1,0:T(8,128)(2,1)} %columns_hbm.1, s32[1,2048]{1,0:T(1,128)} %bitcast.3, ...), custom_call_target="tpu_custom_call" | custom-call | tf_op jit(solution)/shard_map/gather/pallas_call | solution.py:298
  40.4 4.1 %compute.1 = f32[8,64,1024]{2,1,0:T(8,128)} custom-call(bf16[1024,16,128]{2,1,0:T(8,128)(2,1)S(1)} %get-tuple-element.10.c_ref, bf16[1024,2048]{1,0:T(8,128)(2,1)S(1)} %get-tuple-element.11.s_ref, f32[64,8,128]{2,1,0:T(8,128)S(1)} %get-tuple-element.12.k_ref, bf16[3,512,256]{2,1,0:T(8,128)(2,1)S(1)} %get-tuple-element.13.p_ref, ...), custom_call_target="tpu_custom_call" | custom-call | tf_op jit(solution)/shard_map/compute/pallas_call | solution.py:328

commit v4 on v3

--- a/solution.py
+++ b/solution.py
@@ -21,13 +21,13 @@
     return ((lax.div(y, 2) * NZ + z) * 2 + core, lax.rem(y, 2) * NX + x)
 
 
-NEAR = {0: 0, 1: 1, -1: 2}
+NEAR = {0: 0, 1: 1, -1: 2, 2: 3, -2: 4}
 FAR = {
-    2: (0, 0), -2: (0, 1), 3: (0, 2), -3: (0, 3), 4: (0, 4), -4: (0, 5),
+    3: (0, 0), -3: (0, 1), 4: (0, 2), -4: (0, 3),
     5: (1, 0), -5: (1, 1), 6: (1, 2), -6: (1, 3), 7: (1, 4), -7: (1, 5), 8: (1, 6),
 }
-WIDTH = (6, 7)
-BASE = (48, 144)
+WIDTH = (4, 7)
+BASE = (80, 144)
 HALF = 256
 
 
@@ -128,7 +128,7 @@
     def z_send(rel_from, rel_to):
         peer = device(x, y, lax.rem(z - (rel_to - rel_from) + NZ, NZ), core)
         group, slot = FAR[rel_to]
-        at = group * 6 + slot
+        at = group * 4 + slot
         z_copies[rel_to] = [
             send(
                 near(half, 0, ab[half], 1) if rel_from == 0 else far_one(half, rel_from),
@@ -157,7 +157,7 @@
 
     own[0].wait()
     own[1].wait()
-    for rel in (4, -4, 3, -3, 2, -2):
+    for rel in (4, -4, 3, -3):
         z_send(0, rel)
     own_first = spread([near(half, 0, ab[half], 1) for half in (0, 1)], (y_peers, x_peers), fs.at[2], fr.at[2])
 
@@ -224,7 +224,7 @@
             z_send(-4, -rel)
     wait(own_first)
     own_second = spread([near(half, 0, lead[half] * 4, 4) for half in (0, 1)], (x_peers, y_peers), ss.at[2], sr.at[2])
-    for rel in (2, -2, 3, -3):
+    for rel in (3, -3):
         wait(z_copies[rel])
     first_a = first(0)
     wait(row_copies)
@@ -246,16 +246,24 @@
     shared = []
     for i, rel in enumerate((1, -1)):
         wait(plane_copies[rel])
+        peer = device(x, y, lax.rem(z - rel + NZ, NZ), core)
+        plane_copies[2 * rel] = [
+            send(near(half, rel, 0, 16), near(half, 2 * rel, 0, 16), ps.at[2 + i, half], pr.at[2 + i, half], peer)
+            for half in (0, 1)
+        ]
         shared += share(2 + i, [near(half, rel, 0, 16) for half in (0, 1)])
     wait(first_b)
     second_b = second(1)
     wait(second_a)
     shared += share(1, [far(half, 0, 0, 16) for half in (0, 1)])
-    shared_b = share(4, [far(half, 1, lead[half] * 4, 4) for half in (0, 1)])
+    shared_b = share(6, [far(half, 1, lead[half] * 4, 4) for half in (0, 1)])
+    for i, rel in enumerate((2, -2)):
+        wait(plane_copies[rel])
+        shared += share(4 + i, [near(half, rel, 0, 16) for half in (0, 1)])
     p_ref[0] = polar_of(EARLY, core, c_ref, s_ref, w_ref.at[0])
     for at, (i, back) in enumerate(((1, 3), (2, 1), (0, 2))):
         wait(second_b[2 * i : 2 * i + 2])
-        shared_b += share(5 + at, [far(half, 1, lax.rem(lead[half] + back, 4) * 4, 4) for half in (0, 1)])
+        shared_b += share(7 + at, [far(half, 1, lax.rem(lead[half] + back, 4) * 4, 4) for half in (0, 1)])
     p_ref[1] = polar_of(LATE, core, c_ref, s_ref, w_ref.at[1])
     wait(shared)
     p_ref[2] = polar_of(EARLY, 1 - core, c_ref, s_ref, w_ref.at[0])
@@ -274,10 +282,14 @@
     copies = []
     for step in range(4):
         y_hi, part = divmod(step, 2)
-        polar = jnp.dot(l_ref[y_hi], q_ref[part], preferred_element_type=jnp.float32)
+        polar = [
+            jnp.dot(l_ref[y_hi, pl.ds(h * 256, 256)], q_ref[part], preferred_element_type=jnp.float32) for h in range(2)
+        ]
         for rt in range(8):
             for lt in range(2):
-                parts = [polar[j * 64 + rt * 8 : j * 64 + rt * 8 + 8, lt * 128 : lt * 128 + 128] for j in range(8)]
+                parts = [
+                    polar[j // 4][j % 4 * 64 + rt * 8 : j % 4 * 64 + rt * 8 + 8, lt * 128 : lt * 128 + 128] for j in range(8)
+                ]
                 for k in range(8):
                     total = k_ref[k * 8] * parts[0]
                     for j in range(1, 8):
@@ -316,8 +328,8 @@
             pltpu.SMEM((8,), jnp.float32),
             pltpu.SMEM((8,), jnp.float32),
             pltpu.SMEM((8,), jnp.float32),
-            dma((2, 13)), dma((2, 13)), dma((7,)), dma((7,)), dma((3, 2, 3)), dma((3, 2, 3)), dma((3, 2, 3)), dma((3, 2, 3)),
-            dma((2, 2)), dma((2, 2)), dma((8, 2)), dma((8, 2)), dma((9,)),
+            dma((2, 11)), dma((2, 11)), dma((7,)), dma((7,)), dma((3, 2, 3)), dma((3, 2, 3)), dma((3, 2, 3)), dma((3, 2, 3)),
+            dma((4, 2)), dma((4, 2)), dma((10, 2)), dma((10, 2)), dma((9,)),
         ],
         compiler_params=pltpu.CompilerParams(collective_id=0, has_side_effects=True, vmem_limit_bytes=67043328 - 9961472 - 8192),
         name="gather",

time: 44.6 us -> 44 us (0.987)
  Pallas kernels: 44.5 us -> 43.8 us
where the time goes in v4:
time: 44 us; the launch traced here: 43.8 us
  Pallas kernels  43.8 us (100%)
    pallas_call x1, Pallas kernels, body(): pl.pallas_call(gather_kernel, out_shape=(pltpu.VMEM((4 * HALF, 16, 128),...  39.9 us
    pallas_call x1, Pallas kernels, body(): pl.pallas_call(compute_kernel, out_shape=jax.ShapeDtypeStruct((8, 64, 102...  3.88 us

profile of v4, /device:TPU:1, one launch (start us, length us, event | category | flops | bytes accessed | tf_op | source)
XLA Modules:
  0.0 43.8 jit_solution(12594715392158865884)
XLA Ops:
  0.0 39.9 %gather.1 = (bf16[1024,16,128]{2,1,0:T(8,128)(2,1)S(1)}, bf16[1024,2048]{1,0:T(8,128)(2,1)S(1)}, f32[64,8,128]{2,1,0:T(8,128)S(1)}, bf16[3,512,256]{2,1,0:T(8,128)(2,1)S(1)}, bf16[2,512,256]{2,1,0:T(8,128)(2,1)S(1)}) custom-call(bf16[512,256]{1,0:T(8,128)(2,1)} %rows_hbm.1, bf16[16,256]{1,0:T(8,128)(2,1)} %columns_hbm.1, s32[1,2048]{1,0:T(1,128)} %bitcast.3, ...), custom_call_target="tpu_custom_call" | custom-call | tf_op jit(solution)/shard_map/gather/pallas_call | solution.py:310
  40.0 3.9 %compute.1 = f32[8,64,1024]{2,1,0:T(8,128)} custom-call(bf16[1024,16,128]{2,1,0:T(8,128)(2,1)S(1)} %get-tuple-element.10.c_ref, bf16[1024,2048]{1,0:T(8,128)(2,1)S(1)} %get-tuple-element.11.s_ref, f32[64,8,128]{2,1,0:T(8,128)S(1)} %get-tuple-element.12.k_ref, bf16[3,512,256]{2,1,0:T(8,128)(2,1)S(1)} %get-tuple-element.13.p_ref, ...), custom_call_target="tpu_custom_call" | custom-call | tf_op jit(solution)/shard_map/compute/pallas_call | solution.py:340

commit v5 on v4

--- a/solution.py
+++ b/solution.py
@@ -254,9 +254,9 @@
         shared += share(2 + i, [near(half, rel, 0, 16) for half in (0, 1)])
     wait(first_b)
     second_b = second(1)
+    shared_b = share(6, [far(half, 1, lead[half] * 4, 4) for half in (0, 1)])
     wait(second_a)
     shared += share(1, [far(half, 0, 0, 16) for half in (0, 1)])
-    shared_b = share(6, [far(half, 1, lead[half] * 4, 4) for half in (0, 1)])
     for i, rel in enumerate((2, -2)):
         wait(plane_copies[rel])
         shared += share(4 + i, [near(half, rel, 0, 16) for half in (0, 1)])

time: 44 us -> 44 us (level)
  no operation moved by 1% of the time
where the time goes in v5:
time: 44 us; the launch traced here: 43.8 us
  Pallas kernels  43.8 us (100%)
    pallas_call x1, Pallas kernels, body(): pl.pallas_call(gather_kernel, out_shape=(pltpu.VMEM((4 * HALF, 16, 128),...  39.9 us
    pallas_call x1, Pallas kernels, body(): pl.pallas_call(compute_kernel, out_shape=jax.ShapeDtypeStruct((8, 64, 102...  3.88 us

profile of v5, /device:TPU:1, one launch (start us, length us, event | category | flops | bytes accessed | tf_op | source)
XLA Modules:
  0.0 43.8 jit_solution(18400200998937179677)
XLA Ops:
  0.0 39.9 %gather.1 = (bf16[1024,16,128]{2,1,0:T(8,128)(2,1)S(1)}, bf16[1024,2048]{1,0:T(8,128)(2,1)S(1)}, f32[64,8,128]{2,1,0:T(8,128)S(1)}, bf16[3,512,256]{2,1,0:T(8,128)(2,1)S(1)}, bf16[2,512,256]{2,1,0:T(8,128)(2,1)S(1)}) custom-call(bf16[512,256]{1,0:T(8,128)(2,1)} %rows_hbm.1, bf16[16,256]{1,0:T(8,128)(2,1)} %columns_hbm.1, s32[1,2048]{1,0:T(1,128)} %bitcast.3, ...), custom_call_target="tpu_custom_call" | custom-call | tf_op jit(solution)/shard_map/gather/pallas_call | solution.py:310
  40.0 3.9 %compute.1 = f32[8,64,1024]{2,1,0:T(8,128)} custom-call(bf16[1024,16,128]{2,1,0:T(8,128)(2,1)S(1)} %get-tuple-element.10.c_ref, bf16[1024,2048]{1,0:T(8,128)(2,1)S(1)} %get-tuple-element.11.s_ref, f32[64,8,128]{2,1,0:T(8,128)S(1)} %get-tuple-element.12.k_ref, bf16[3,512,256]{2,1,0:T(8,128)(2,1)S(1)} %get-tuple-element.13.p_ref, ...), custom_call_target="tpu_custom_call" | custom-call | tf_op jit(solution)/shard_map/compute/pallas_call | solution.py:340
